TPU v7x, 32 devices: a whole 2x2x4 slice. The times are simulated.
32 devices in a mesh: gx: 4 (over x, core), gy: 8 (over z, y).
Axes of the slice: x: 2, y: 2, z: 4, core: 2. Of those that a mesh axis runs over, the one named last changes fastest.
Arguments:
- queries: bfloat16 [256, 2560], P('gx'), may hold values from -8 to 8
- token_key_value: bfloat16 [256, 1024], P('gx'), may hold values from -6 to 6
- group_cached_keys: bfloat16 [4, 32768, 512], P('gx', 'gy'), may hold values from -8 to 8
- group_cached_values: bfloat16 [4, 32768, 512], P('gx', 'gy'), may hold values from -6 to 6
- owners: int32 [4, 32768], P('gx', 'gy'), may hold values from 0 to 63, never falling along the last dimension, each value on 1 to 16384 neighbouring positions
- out_weight: bfloat16 [2560, 2560], P(None, 'gy'), may hold values from -0.125 to 0.125
- residual: bfloat16 [256, 2560], P('gx', 'gy'), may hold values from -6 to 6
- norm_gain: bfloat16 [2560], P('gy'), may hold values from 0.099609375 to 1.8984375
- expert_ids: int32 [256, 6], replicated, may hold values from 0 to 63, all different within a row; in each aligned block of 64 rows (0 to 63, 64 to 127, ...) at most 12 rows name the same one
- gate_logits: float32 [256, 6], replicated, may hold values from -0.5 to 0.5
- w_gate_up: bfloat16 [64, 2560, 3072], P('gx', 'gy'), may hold values from -0.125 to 0.125
- w_down: bfloat16 [64, 1536, 2560], P('gx', None, 'gy'), may hold values from -0.15625 to 0.15625
Outputs:
- layer_out: float32 [256, 2560], P('gx', 'gy')
Inputs may be any that keep to these rules, and one draw needn't show every extreme that they name: `owners`: each request's positions form one run; every request owns at least one position and at most 16384, and some request owns exactly 16384. `expert_ids`: within each group of 64 requests no expert is named by more than 12 requests, a bound that some block reaches.
All inputs are finite; a program needn't handle non-finite values.
Results may differ from a plain program's by a relative error of at most 0.0075.
Values may be sent and summed in bfloat16 or wider, within the bound.
No kernel may reach another device: no remote copies, remote signals or barrier semaphores. Data moves between devices by JAX's collectives and lax.ppermute only.
A program may use at most 192 MiB of HBM per device.

v0:
```python
import jax
import jax.numpy as jnp
from jax import lax
from jax.sharding import PartitionSpec as P

D = 2560
QUERY_HEADS = 20
KEY_VALUE_HEADS = 4
HEAD_SIZE = 128
E = 64
TOPK = 6
CAPS = 12
minimal_score = -1e30
norm_epsilon = 1e-05


def merged(part, axis, combine):
    gathered = jax.tree.map(lambda a: lax.all_gather(a, axis), part)

    def take(source):
        return jax.tree.map(lambda a: lax.dynamic_index_in_dim(a, source, 0, False), gathered)

    return lax.fori_loop(
        1, lax.axis_size(axis), lambda source, state: combine(state, take(source)), take(0)
    )


def merge_partial(earlier_part, later_part):
    max_one, den_one, acc_one = earlier_part
    max_two, den_two, acc_two = later_part
    peak = jnp.maximum(max_one, max_two)
    scale_one = jnp.exp(max_one - peak)
    scale_two = jnp.exp(max_two - peak)
    return (
        peak,
        den_one * scale_one + den_two * scale_two,
        acc_one * scale_one[..., None] + acc_two * scale_two[..., None],
    )


def slot_ranks(flat_ids, num_experts):
    onehot = (flat_ids[..., None] == lax.iota(jnp.int32, num_experts)).astype(jnp.int32)
    earlier = jnp.cumsum(onehot, axis=-2) - onehot
    return jnp.sum(earlier * onehot, axis=-1)


def attend_local(queries, group_cached_keys, group_cached_values, owners):
    request_rows = queries.shape[0]
    query_heads_per_group = QUERY_HEADS // KEY_VALUE_HEADS
    positions = group_cached_keys.shape[0]
    block_length = min(positions, 512)
    block_count = positions // block_length
    key_block_list = group_cached_keys.reshape(
        block_count, block_length, KEY_VALUE_HEADS, HEAD_SIZE
    )
    value_block_list = group_cached_values.reshape(
        block_count, block_length, KEY_VALUE_HEADS, HEAD_SIZE
    )
    owner_blocks = owners.reshape(block_count, block_length)
    scaling = HEAD_SIZE ** (-0.5)
    request_ids = lax.iota(jnp.int32, request_rows)

    def visit_block(state_in, inputs):
        run_max, run_den, run_acc = state_in
        key_block, value_block, owning_block = inputs
        picked_experts = queries[owning_block].reshape(
            block_length, KEY_VALUE_HEADS, query_heads_per_group, HEAD_SIZE
        )
        scores = (
            jnp.einsum(
                "tkgd,tkd->tkg", picked_experts, key_block, preferred_element_type=jnp.float32
            )
            * scaling
        )
        member = owning_block[:, None] == request_ids[None, :]
        block_max = jnp.max(
            jnp.where(member[:, :, None, None], scores[:, None], minimal_score), axis=0
        )
        new_max = jnp.maximum(run_max, block_max)
        prob_block = jnp.exp(scores - new_max[owning_block]).astype(jnp.bfloat16)
        spread = jnp.where(
            member[:, :, None, None], prob_block[:, None], jnp.zeros((), jnp.bfloat16)
        )
        rescale = jnp.exp(run_max - new_max)
        run_den = run_den * rescale + jnp.sum(spread.astype(jnp.float32), axis=0)
        run_acc = run_acc * rescale[..., None] + jnp.einsum(
            "trkg,tkd->rkgd", spread, value_block, preferred_element_type=jnp.float32
        )
        return ((new_max, run_den, run_acc), None)

    initial = (
        jnp.full(
            (request_rows, KEY_VALUE_HEADS, query_heads_per_group), minimal_score, jnp.float32
        ),
        jnp.zeros((request_rows, KEY_VALUE_HEADS, query_heads_per_group), jnp.float32),
        jnp.zeros((request_rows, KEY_VALUE_HEADS, query_heads_per_group, HEAD_SIZE), jnp.float32),
    )
    return lax.scan(visit_block, initial, (key_block_list, value_block_list, owner_blocks))[0]


def expert_block(tokens, w_gate_up, w_down):
    hidden_units = w_down.shape[1]
    gate_up = jnp.einsum("sekd,edf->sekf", tokens, w_gate_up, preferred_element_type=jnp.float32)
    gate_up = lax.psum(gate_up, "gy")
    active = (jax.nn.silu(gate_up[..., :hidden_units]) * gate_up[..., hidden_units:]).astype(
        jnp.bfloat16
    )
    return jnp.einsum("sekf,efd->sekd", active, w_down, preferred_element_type=jnp.float32).astype(
        jnp.bfloat16
    )


def shards(
    queries,
    token_key_value,
    group_cached_keys,
    group_cached_values,
    owners,
    out_weight,
    residual,
    norm_gain,
    expert_ids,
    gate_logits,
    w_gate_up,
    w_down,
):
    request_rows = queries.shape[0]
    query_heads_per_group = QUERY_HEADS // KEY_VALUE_HEADS
    key_value_width = token_key_value.shape[1] // 2
    scaling = HEAD_SIZE ** (-0.5)
    run_max, run_den, run_acc = attend_local(
        queries, group_cached_keys[0], group_cached_values[0], owners[0]
    )
    query_head_rows = queries.reshape(
        request_rows, KEY_VALUE_HEADS, query_heads_per_group, HEAD_SIZE
    )
    appended_keys = token_key_value[:, :key_value_width].reshape(
        request_rows, KEY_VALUE_HEADS, HEAD_SIZE
    )
    appended_values = token_key_value[:, key_value_width:]
    own_score = (
        jnp.einsum(
            "rkgd,rkd->rkg", query_head_rows, appended_keys, preferred_element_type=jnp.float32
        )
        * scaling
    )
    run_max, run_den, run_acc = merged((run_max, run_den, run_acc), "gy", merge_partial)
    peak = jnp.maximum(run_max, own_score)
    rescale = jnp.exp(run_max - peak)
    own_prob = lax.optimization_barrier(jnp.exp(own_score - peak).astype(jnp.bfloat16)).astype(
        jnp.float32
    )
    denominator = run_den * rescale + own_prob
    incoming_values = appended_values.astype(jnp.float32).reshape(
        request_rows, KEY_VALUE_HEADS, 1, HEAD_SIZE
    )
    numerator = run_acc * rescale[..., None] + own_prob[..., None] * incoming_values
    attention = (
        (numerator / denominator[..., None])
        .astype(jnp.bfloat16)
        .reshape(request_rows, QUERY_HEADS * HEAD_SIZE)
    )
    projected = jnp.dot(attention, out_weight, preferred_element_type=jnp.float32)
    hidden = (residual.astype(jnp.float32) + projected).astype(jnp.bfloat16)
    hidden_f = hidden.astype(jnp.float32)
    squares = lax.psum(jnp.sum(hidden_f * hidden_f, axis=1), "gy")
    inv_rms = lax.rsqrt(squares / D + norm_epsilon)
    normed = (hidden_f * inv_rms[:, None] * norm_gain.astype(jnp.float32)[None, :]).astype(
        jnp.bfloat16
    )
    mixing = jax.nn.softmax(gate_logits, axis=-1)
    num_gx = lax.axis_size("gx")
    group_index = lax.axis_index("gx")
    per_row = w_gate_up.shape[0]
    columns_here = normed.shape[1]
    my_ids = lax.dynamic_slice_in_dim(
        expert_ids, group_index * request_rows, request_rows, 0
    ).reshape(-1)
    my_mix = lax.dynamic_slice_in_dim(mixing, group_index * request_rows, request_rows, 0)
    places = my_ids * CAPS + slot_ranks(my_ids, E)
    outgoing = (
        jnp.zeros((E * CAPS, columns_here), jnp.bfloat16)
        .at[places]
        .set(jnp.repeat(normed, TOPK, axis=0))
    )
    returned = lax.all_to_all(
        expert_block(
            lax.all_to_all(
                outgoing.reshape(num_gx, per_row, CAPS, columns_here),
                "gx",
                split_axis=0,
                concat_axis=0,
                tiled=True,
            ),
            w_gate_up,
            w_down,
        ),
        "gx",
        split_axis=0,
        concat_axis=0,
        tiled=True,
    )
    picked = (
        returned.reshape(E * CAPS, columns_here)[places]
        .astype(jnp.float32)
        .reshape(request_rows, TOPK, columns_here)
    )
    routed = jnp.sum(my_mix[..., None] * picked, axis=1)
    return hidden_f + routed


def solution(mesh):
    placed = (
        P("gx", None),
        P("gx", None),
        P("gx", "gy", None),
        P("gx", "gy", None),
        P("gx", "gy"),
        P(None, "gy"),
        P("gx", "gy"),
        P("gy"),
        P(),
        P(),
        P("gx", "gy", None),
        P("gx", None, "gy"),
    )
    return jax.shard_map(
        shards, mesh=mesh, in_specs=placed, out_specs=P("gx", "gy"), check_vma=False
    )
```

profile of v0, /device:TPU:0, one launch (start us, length us, event | category | flops | bytes accessed | tf_op | source)
XLA Modules:
  0.0 817.4 jit_solution(4890092526414652480)
XLA Ops:
  6.5 7.0 reshape.208
  13.6 7.0 reshape_squeeze.10
  22.4 178.0 %while.35 = (s32[]{:T(128)}, f32[64,4,5]{2,1,0:T(4,128)S(1)}, f32[64,4,5]{2,1,0:T(4,128)S(1)}, f32[64,4,5,128]{3,0,2,1:T(8,128)}, s32[8,512]{1,0:T(8,128)}, /*in...) while((s32[]{:T(128)}, f32[64,4,5]{2,1,0:T(4,128)S(1)}, ...), condition=%wide.region_3.4_spmd.clone, body=%wide.region_0.3_spmd.clone.sunk | while | flops 176462592 | bytes 21555320 | solution.py:98
  23.1 3.6 gather_fusion
  26.7 4.5 copy.169
  44.4 3.6 gather_fusion
  48.0 4.5 copy.169
  66.8 3.6 gather_fusion
  70.4 4.5 copy.169
  86.0 2.4 fusion.70
  89.2 3.6 gather_fusion
  92.8 4.5 copy.169
  108.4 2.4 fusion.70
  111.6 3.6 gather_fusion
  115.2 4.5 copy.169
  134.0 3.6 gather_fusion
  137.6 4.5 copy.169
  156.4 3.6 gather_fusion
  160.0 4.5 copy.169
  178.8 3.6 gather_fusion
  182.4 4.5 copy.169
  202.2 38.6 %all-gather = f32[512,4,5]{2,1,0:T(4,128)S(1)} all-gather(f32[64,4,5]{2,1,0:T(4,128)S(1)} %get-tuple-element.232), channel_id=2, replica_groups=mesh['gx'=4,'gy'=8] {'gy'}, dimensions={0}, use_global_device_ids=true | all-gather | bytes 46080 | tf_op jit(solution)/shard_map/all_gather | solution.py:18
  240.9 35.2 %all-gather.1 = f32[512,4,5]{2,1,0:T(4,128)S(1)} all-gather(f32[64,4,5]{2,1,0:T(4,128)S(1)} %get-tuple-element.233), channel_id=3, replica_groups=mesh['gx'=4,'gy'=8] {'gy'}, dimensions={0}, use_global_device_ids=true | all-gather | bytes 46080 | tf_op jit(solution)/shard_map/all_gather | solution.py:18
  282.6 27.2 %all-gather.5.cloned.1.call-done = f32[512,4,5,128]{3,0,2,1:T(8,128)} async-done(((f32[64,4,5,128]{3,0,2,1:T(8,128)}), f32[512,4,5,128]{3,0,2,1:T(8,128)}) %all-gather.5.cloned.1.call-update) | async-done | bytes 5242896 | tf_op jit(solution)/shard_map/all_gather | solution.py:18
  311.4 20.6 %while.34 = (s32[]{:T(128)}, f32[64,4,5]{0,1,2:T(4,128)S(1)}, f32[64,4,5]{0,1,2:T(4,128)S(1)}, f32[64,4,5,128]{3,2,1,0:T(8,128)S(1)}, f32[8,64,4,5]{1,2,3,0:T(4,...) while((s32[]{:T(128)}, f32[64,4,5]{0,1,2:T(4,128)S(1)}, ...), condition=%wide.region_5.6_spmd, body=%wide.region_4.5_spmd.sunk | while | flops 499205 | bytes 3348631 | solution.py:23
  336.7 19.3 %psum.14 = f32[64]{0:T(128)S(1)} all-reduce(f32[64]{0:T(128)S(1)} %get-tuple-element.365), channel_id=1, replica_groups=mesh['gx'=4,'gy'=8] {'gy'}, use_global_device_ids=true, to_apply=%region_12.13 | all-reduce | flops 64 | bytes 512 | tf_op jit(solution)/shard_map/psum | solution.py:166
  358.7 12.1 %all_to_all.10 = bf16[4,16,12,320]{3,1,2,0:T(8,128)(2,1)S(1)} all-to-all(bf16[4,16,12,320]{3,1,2,0:T(8,128)(2,1)S(1)} %copy.108), channel_id=1, replica_groups=mesh['gx'=4,'gy'=8] {'gx'}, dimensions={0} | all-to-all | bytes 983040 | tf_op jit(solution)/shard_map/all_to_all | solution.py:188
  370.8 16.6 %fusion.23 = f32[4,16,12,3072]{3,2,0,1:T(8,128)} fusion(bf16[16,320,3072]{2,1,0:T(8,128)(2,1)} %param.26, bf16[4,16,12,320]{3,1,2,0:T(8,128)(2,1)S(1)} %all_to_all.10), kind=kOutput, calls=%fused_computation.44 | convolution fusion | flops 1509949440 | bytes 41385984 | tf_op jit(solution)/shard_map/sekd,edf->sekf/dot_general | solution.py:103
  388.2 393.0 %all-reduce.2.cloned.1.call-done = f32[4,16,12,3072]{3,2,0,1:T(8,128)} async-done(((f32[4,16,12,3072]{3,2,0,1:T(8,128)}), f32[4,16,12,3072]{3,2,0,1:T(8,128)}) %all-reduce.2.cloned.1.call-update) | async-done | bytes 9437200 | tf_op jit(solution)/shard_map/psum | solution.py:104
  781.2 11.6 %fusion.34 = bf16[4,16,12,320]{3,2,0,1:T(8,128)(2,1)S(1)} fusion(bf16[16,1536,320]{1,2,0:T(8,128)(2,1)} %param.27, f32[4,16,12,3072]{3,2,0,1:T(8,128)} %all-reduce.2.cloned.1.call-done), kind=kOutput, calls=%fused_computation.49 | convolution fusion | flops 762298368 | bytes 25657344 | tf_op jit(solution)/shard_map/sekf,efd->sekd/dot_general | solution.py:108
  793.9 3.5 all-to-all-start.1
  797.7 9.2 %all-to-all-done.1 = bf16[4,16,12,320]{3,1,2,0:T(8,128)(2,1)S(1)} async-done(((bf16[4,16,12,320]{3,1,2,0:T(8,128)(2,1)}), bf16[4,16,12,320]{3,1,2,0:T(8,128)(2,1)S(1)}, u32[]{:S(2)}, u32[]{:S(2)}) %all-to-all-start.1) | async-done | bytes 491552 | tf_op jit(solution)/shard_map/all_to_all | solution.py:186
  (292 shorter events, 152.7 us)
Async XLA Ops:
  6.5 329.4 %copy-start = (bf16[2560,320]{0,1:T(8,128)(2,1)S(1)}, bf16[2560,320]{0,1:T(8,128)(2,1)}, u32[]{:S(2)}) copy-start(bf16[2560,320]{0,1:T(8,128)(2,1)} %param.21) | copy-start | bytes 4915204
  6.5 303.3 %all-gather.5.cloned.1.call-start = ((), (), s32[]{:S(2)}) async-start(), calls=%async_computation.3 | async-start | bytes 5898240 | tf_op jit(solution)/shard_map/all_gather | solution.py:18
  13.6 7.5 copy-start.6
  13.6 8.8 %copy-start.1 = (bf16[64,2560]{1,0:T(8,128)(2,1)S(1)}, bf16[64,2560]{1,0:T(8,128)(2,1)}, u32[]{:S(2)}) copy-start(bf16[64,2560]{1,0:T(8,128)(2,1)} %param.16) | copy-start | bytes 983044
  22.4 179.4 %copy-start.7 = (s32[256,6]{0,1:T(8,128)S(1)}, s32[256,6]{0,1:T(8,128)}, u32[]{:S(2)}) copy-start(s32[256,6]{0,1:T(8,128)} %param.24) | copy-start | bytes 18436
  200.4 78.9 %copy-start.3 = (bf16[64,1024]{1,0:T(8,128)(2,1)S(1)}, bf16[64,1024]{1,0:T(8,128)(2,1)}, u32[]{:S(2)}) copy-start(bf16[64,1024]{1,0:T(8,128)(2,1)} %param.17) | copy-start | bytes 393220
  200.5 80.5 %copy-start.8 = (bf16[320]{0:T(512)(128)(2,1)S(1)}, bf16[320]{0:T(512)(128)(2,1)}, u32[]{:S(2)}) copy-start(bf16[320]{0:T(512)(128)(2,1)} %param.23) | copy-start | bytes 1924
  200.5 580.7 %all-reduce.2.cloned.1.call-start = ((), (), s32[]{:S(2)}) async-start(), calls=%async_computation.2 | async-start | bytes 25165824 | tf_op jit(solution)/shard_map/psum | solution.py:104
  276.2 1.0 copy-start.2
  311.4 24.6 %copy-start.4 = (bf16[64,320]{1,0:T(8,128)(2,1)S(1)}, bf16[64,320]{1,0:T(8,128)(2,1)}, u32[]{:S(2)}) copy-start(bf16[64,320]{1,0:T(8,128)(2,1)} %param.22) | copy-start | bytes 122884
  387.4 0.7 copy-start.5
  793.9 13.0 %all-to-all-start.1 = ((bf16[4,16,12,320]{3,1,2,0:T(8,128)(2,1)}), bf16[4,16,12,320]{3,1,2,0:T(8,128)(2,1)S(1)}, u32[]{:S(2)}, u32[]{:S(2)}) async-start(bf16[4,16,12,320]{3,1,2,0:T(8,128)(2,1)} %copy.110), calls=%async_computation.1 | async-start | bytes 1179648 | tf_op jit(solution)/shard_map/all_to_all | solution.py:186
Sparse Core Ops, SparseCore 0:
  200.6 109.1 all-gather.4
  387.6 393.5 all-reduce.1
where the time goes:
time: 821 us; the launch traced here: 817 us
  waiting for transfers between devices  429 us (52%)
  local copies, waits for them, and re-layouts  151 us (18%)
  blocking collectives  105 us (13%)
  other arithmetic  64.6 us (8%)
  matrix products  48.9 us (6%)
  between operations  13.7 us (2%)
    psum x1, waiting for transfers between devices, expert_block(): gate_up = lax.psum(gate_up, 'gy')  393 us
    all_gather x2, blocking collectives, merged(): gathered = jax.tree.map(lambda a: lax.all_gather(a, axis), part)  73.9 us
    while x24, local copies, waits for them, and re-layouts  48.4 us
    while x16, other arithmetic  35.7 us
    gather x8, local copies, waits for them, and re-layouts, visit_block(): queries[owning_block]  28.5 us
    all_gather x1, waiting for transfers between devices, merged(): gathered = jax.tree.map(lambda a: lax.all_gather(a, axis), part)  27.2 us
    gather x16, local copies, waits for them, and re-layouts, visit_block(): prob_block = jnp.exp(scores - new_max[owning_block]).astype(jnp.bfloat16)  19.4 us
    psum x1, blocking collectives, shards(): squares = lax.psum(jnp.sum(hidden_f * hidden_f, axis=1), 'gy')  19.3 us
  transfers between devices with their start and end apart: 3, of which 3 were waited for; matrix products, arithmetic and copies ran while one was open for 1% of the time, Pallas kernels for 0%

commit v1 on v0

--- a/solution.py
+++ b/solution.py
@@ -101,7 +101,12 @@
 def expert_block(tokens, w_gate_up, w_down):
     hidden_units = w_down.shape[1]
     gate_up = jnp.einsum("sekd,edf->sekf", tokens, w_gate_up, preferred_element_type=jnp.float32)
-    gate_up = lax.psum(gate_up, "gy")
+    size = lax.axis_size("gy")
+    total, far = (gate_up, 1)
+    while far < size:
+        total = total + lax.ppermute(total, "gy", [(i, i ^ far) for i in range(size)])
+        far = 2 * far
+    gate_up = total
     active = (jax.nn.silu(gate_up[..., :hidden_units]) * gate_up[..., hidden_units:]).astype(
         jnp.bfloat16
     )

time: 821 us -> 1320 us (1.61)
  waiting for transfers between devices: 429 us -> 851 us
  other arithmetic: 64.6 us -> 113 us
    ppermute x0 -> x3, waiting for transfers between devices: none -> 815 us  [expert_block(): lax.ppermute(total, 'gy', [(i, i ^ far) for i in range(size)])]
    psum x1 -> x0, waiting for transfers between devices: 393 us -> none  [expert_block(): gate_up = lax.psum(gate_up, 'gy')]
    add x0 -> x3, other arithmetic: none -> 43 us  [expert_block(): total + lax.ppermute(total, 'gy', [(i, i ^ far) for i in range(size)])]
  transfers between devices with their start and end apart: 3 -> 5, of which waited for: 3 -> 5; matrix products, arithmetic and copies ran while one was open for 1% -> 1% of each run, Pallas kernels for 0% -> 0%
where the time goes in v1:
time: 1320 us; the launch traced here: 1310 us
  waiting for transfers between devices  851 us (64%)
  local copies, waits for them, and re-layouts  160 us (12%)
  blocking collectives  117 us (9%)
  other arithmetic  113 us (9%)
  matrix products  48.3 us (4%)
  between operations  14.1 us (1%)
    ppermute x3, waiting for transfers between devices, expert_block(): lax.ppermute(total, 'gy', [(i, i ^ far) for i in range(size)])  815 us
    all_gather x2, blocking collectives, merged(): gathered = jax.tree.map(lambda a: lax.all_gather(a, axis), part)  74 us
    while x24, local copies, waits for them, and re-layouts  48.4 us
    add x3, other arithmetic, expert_block(): total + lax.ppermute(total, 'gy', [(i, i ^ far) for i in range(size)])  43 us
    while x16, other arithmetic  35.7 us
    psum x1, blocking collectives, shards(): squares = lax.psum(jnp.sum(hidden_f * hidden_f, axis=1), 'gy')  30.7 us
    gather x8, local copies, waits for them, and re-layouts, visit_block(): queries[owning_block]  28.5 us
    all_gather x1, waiting for transfers between devices, merged(): gathered = jax.tree.map(lambda a: lax.all_gather(a, axis), part)  27.1 us
  transfers between devices with their start and end apart: 5, of which 5 were waited for; matrix products, arithmetic and copies ran while one was open for 1% of the time, Pallas kernels for 0%

profile of v1, /device:TPU:0, one launch (start us, length us, event | category | flops | bytes accessed | tf_op | source)
XLA Modules:
  0.0 1308.7 jit_solution(2745890074976167250)
XLA Ops:
  6.5 7.0 reshape.208
  13.6 7.0 reshape_squeeze.10
  22.4 178.1 %while.35 = (s32[]{:T(128)}, f32[64,4,5]{2,1,0:T(4,128)S(1)}, f32[64,4,5]{2,1,0:T(4,128)S(1)}, f32[64,4,5,128]{3,0,2,1:T(8,128)}, s32[8,512]{1,0:T(8,128)}, /*in...) while((s32[]{:T(128)}, f32[64,4,5]{2,1,0:T(4,128)S(1)}, ...), condition=%wide.region_3.4_spmd.clone, body=%wide.region_0.3_spmd.clone.sunk | while | flops 176462592 | bytes 21555320 | solution.py:98
  23.1 3.6 gather_fusion
  26.7 4.5 copy.187
  44.4 3.6 gather_fusion
  48.0 4.5 copy.187
  66.8 3.6 gather_fusion
  70.4 4.5 copy.187
  89.2 3.6 gather_fusion
  92.8 4.5 copy.187
  115.2 4.5 copy.187
  137.6 4.5 copy.187
  160.0 4.5 copy.187
  182.4 4.5 copy.187
  202.1 38.6 %all-gather = f32[512,4,5]{2,1,0:T(4,128)S(1)} all-gather(f32[64,4,5]{2,1,0:T(4,128)S(1)} %get-tuple-element.232), channel_id=2, replica_groups=mesh['gx'=4,'gy'=8] {'gy'}, dimensions={0}, use_global_device_ids=true | all-gather | bytes 46080 | tf_op jit(solution)/shard_map/all_gather | solution.py:18
  240.9 35.4 %all-gather.1 = f32[512,4,5]{2,1,0:T(4,128)S(1)} all-gather(f32[64,4,5]{2,1,0:T(4,128)S(1)} %get-tuple-element.233), channel_id=3, replica_groups=mesh['gx'=4,'gy'=8] {'gy'}, dimensions={0}, use_global_device_ids=true | all-gather | bytes 46080 | tf_op jit(solution)/shard_map/all_gather | solution.py:18
  282.7 27.1 %all-gather.5.cloned.1.call-done = f32[512,4,5,128]{3,0,2,1:T(8,128)} async-done(((f32[64,4,5,128]{3,0,2,1:T(8,128)}), f32[512,4,5,128]{3,0,2,1:T(8,128)}) %all-gather.5.cloned.1.call-update) | async-done | bytes 5242896 | tf_op jit(solution)/shard_map/all_gather | solution.py:18
  311.3 20.6 %while.34 = (s32[]{:T(128)}, f32[64,4,5]{0,1,2:T(4,128)S(1)}, f32[64,4,5]{0,1,2:T(4,128)S(1)}, f32[64,4,5,128]{3,2,1,0:T(8,128)S(1)}, f32[8,64,4,5]{1,2,3,0:T(4,...) while((s32[]{:T(128)}, f32[64,4,5]{0,1,2:T(4,128)S(1)}, ...), condition=%wide.region_5.6_spmd, body=%wide.region_4.5_spmd.sunk | while | flops 499205 | bytes 3348631 | solution.py:23
  336.6 30.7 %psum.7 = f32[64]{0:T(128)S(1)} all-reduce(f32[64]{0:T(128)S(1)} %get-tuple-element.365), channel_id=1, replica_groups=mesh['gx'=4,'gy'=8] {'gy'}, use_global_device_ids=true, to_apply=%region_12.13 | all-reduce | flops 64 | bytes 512 | tf_op jit(solution)/shard_map/psum | solution.py:171
  370.1 12.3 all_to_all.10
  382.4 16.7 %fusion.19 = f32[16,4,12,3072]{3,2,1,0:T(8,128)} fusion(bf16[16,320,3072]{2,1,0:T(8,128)(2,1)} %param.26, bf16[4,16,12,320]{3,1,2,0:T(8,128)(2,1)S(1)} %all_to_all.10), kind=kOutput, calls=%fused_computation.40 | convolution fusion | flops 1509949440 | bytes 41385984 | tf_op jit(solution)/shard_map/sekd,edf->sekf/dot_general | solution.py:103
  399.1 10.0 copy.166
  409.2 204.7 %collective-permute-done = f32[4,16,12,3072]{3,1,2,0:T(8,128)} collective-permute-done((f32[4,16,12,3072]{3,1,2,0:T(8,128)S(1)}, f32[4,16,12,3072]{3,1,2,0:T(8,128)}, u32[]{:S(2)}, u32[]{:S(2)}) %collective-permute-start) | collective-permute-done | bytes 9437216 | tf_op jit(solution)/shard_map/ppermute | solution.py:107
  613.9 17.4 %fusion.56 = f32[4,16,12,3072]{3,1,2,0:T(8,128)} fusion(f32[4,16,12,3072]{3,1,2,0:T(8,128)} %collective-permute-done, f32[16,4,12,3072]{3,2,1,0:T(8,128)} %fusion.19), kind=kLoop, calls=%fused_computation.87 | loop fusion | flops 2359296 | bytes 28311552 | tf_op jit(solution)/shard_map/add | solution.py:107
  631.4 204.0 %collective-permute-done.1 = f32[4,16,12,3072]{3,1,2,0:T(8,128)} collective-permute-done((f32[4,16,12,3072]{3,1,2,0:T(8,128)}, f32[4,16,12,3072]{3,1,2,0:T(8,128)}, u32[]{:S(2)}, u32[]{:S(2)}) %collective-permute-start.1) | collective-permute-done | bytes 9437216 | tf_op jit(solution)/shard_map/ppermute | solution.py:107
  835.4 12.8 add.147
  848.2 406.2 %collective-permute-done.2 = f32[4,16,12,3072]{3,1,2,0:T(8,128)} collective-permute-done((f32[4,16,12,3072]{3,1,2,0:T(8,128)}, f32[4,16,12,3072]{3,1,2,0:T(8,128)}, u32[]{:S(2)}, u32[]{:S(2)}) %collective-permute-start.2) | collective-permute-done | bytes 9437216 | tf_op jit(solution)/shard_map/ppermute | solution.py:107
  1254.4 12.8 add.148
  1267.1 5.5 fusion.23
  1272.7 11.0 fusion.30
  1288.6 9.2 all-to-all-done.1
  (302 shorter events, 174.7 us)
Async XLA Ops:
  6.5 329.4 %copy-start = (bf16[2560,320]{0,1:T(8,128)(2,1)S(1)}, bf16[2560,320]{0,1:T(8,128)(2,1)}, u32[]{:S(2)}) copy-start(bf16[2560,320]{0,1:T(8,128)(2,1)} %param.21) | copy-start | bytes 4915204
  6.5 303.2 %all-gather.5.cloned.1.call-start = ((), (), s32[]{:S(2)}) async-start(), calls=%async_computation.2 | async-start | bytes 5898240 | tf_op jit(solution)/shard_map/all_gather | solution.py:18
  13.6 7.5 copy-start.7
  13.6 8.8 copy-start.2
  22.4 179.3 %copy-start.8 = (s32[256,6]{0,1:T(8,128)S(1)}, s32[256,6]{0,1:T(8,128)}, u32[]{:S(2)}) copy-start(s32[256,6]{0,1:T(8,128)} %param.24) | copy-start | bytes 18436
  200.4 78.9 %copy-start.4 = (bf16[64,1024]{1,0:T(8,128)(2,1)S(1)}, bf16[64,1024]{1,0:T(8,128)(2,1)}, u32[]{:S(2)}) copy-start(bf16[64,1024]{1,0:T(8,128)(2,1)} %param.17) | copy-start | bytes 393220
  200.5 80.6 %copy-start.9 = (bf16[320]{0:T(512)(128)(2,1)S(1)}, bf16[320]{0:T(512)(128)(2,1)}, u32[]{:S(2)}) copy-start(bf16[320]{0:T(512)(128)(2,1)} %param.23) | copy-start | bytes 1924
  276.2 1.0 copy-start.3
  311.3 24.6 %copy-start.5 = (bf16[64,320]{1,0:T(8,128)(2,1)S(1)}, bf16[64,320]{1,0:T(8,128)(2,1)}, u32[]{:S(2)}) copy-start(bf16[64,320]{1,0:T(8,128)(2,1)} %param.22) | copy-start | bytes 122884
  409.2 204.8 %collective-permute-start = (f32[4,16,12,3072]{3,1,2,0:T(8,128)S(1)}, f32[4,16,12,3072]{3,1,2,0:T(8,128)}, u32[]{:S(2)}, u32[]{:S(2)}) collective-permute-start(f32[4,16,12,3072]{3,1,2,0:T(8,128)S(1)} %bitcast.111), channel_id=1, source_target_pairs={{0,1},{1,0},{2,3},{3,2},{4,5},{5,4},{6,7},{7,6},{8,9},{9,8},{10,11... | collective-permute-start | bytes 28311560 | tf_op jit(solution)/shard_map/ppermute | solution.py:107
  631.4 216.8 %copy-start.6 = (f32[256,6]{0,1:T(8,128)S(1)}, f32[256,6]{0,1:T(8,128)}, u32[]{:S(2)}) copy-start(f32[256,6]{0,1:T(8,128)} %param.25) | copy-start | bytes 18436
  631.4 204.0 %collective-permute-start.1 = (f32[4,16,12,3072]{3,1,2,0:T(8,128)}, f32[4,16,12,3072]{3,1,2,0:T(8,128)}, u32[]{:S(2)}, u32[]{:S(2)}) collective-permute-start(f32[4,16,12,3072]{3,1,2,0:T(8,128)} %fusion.56), channel_id=1, source_target_pairs={{0,2},{1,3},{2,0},{3,1},{4,6},{5,7},{6,4},{7,5},{8,10},{9,11},{10,... | collective-permute-start | bytes 28311560 | tf_op jit(solution)/shard_map/ppermute | solution.py:107
  848.1 406.2 %collective-permute-start.2 = (f32[4,16,12,3072]{3,1,2,0:T(8,128)}, f32[4,16,12,3072]{3,1,2,0:T(8,128)}, u32[]{:S(2)}, u32[]{:S(2)}) collective-permute-start(f32[4,16,12,3072]{3,1,2,0:T(8,128)} %add.147), channel_id=1, source_target_pairs={{0,4},{1,5},{2,6},{3,7},{4,0},{5,1},{6,2},{7,3},{8,12},{9,13},{10,... | collective-permute-start | bytes 28311560 | tf_op jit(solution)/shard_map/ppermute | solution.py:107
  1283.7 17.8 %copy-start.1 = (bf16[2560,320]{0,1:T(8,128)(2,1)S(1)}, bf16[2560,320]{0,1:T(8,128)(2,1)}, u32[]{:S(2)}) copy-start(bf16[2560,320]{0,1:T(8,128)(2,1)} %param.21) | copy-start | bytes 4915204
  1284.9 13.0 all-to-all-start.1
Sparse Core Ops, SparseCore 0:
  200.6 109.1 all-gather.4
